TPU v7x, 256 devices: a whole 4x4x8 slice. The times are simulated.
256 devices in a mesh: grp: 4 (over x), dev: 64 (over y, z, core).
Axes of the slice: x: 4, y: 4, z: 8, core: 2. Of those that a mesh axis runs over, the one named last changes fastest.
Arguments:
- positions: float32 [3, 65536], P(None, ('grp', 'dev')), may hold values from -1 to 1
- velocities: float32 [3, 65536], P(None, ('grp', 'dev')), may hold values from -4 to 4
- accel_old: float32 [3, 65536], P(None, ('grp', 'dev')), may hold values from -6 to 6
- jerk_old: float32 [3, 65536], P(None, ('grp', 'dev')), may hold values from -6 to 6
- masses: float32 [65536], P(('grp', 'dev')), may hold values from 3.0517579e-06 to 7.6293945e-05
- levels: int32 [65536], P(('grp', 'dev')), may hold values from 0 to 3
- live_count: int32 [256], P(('grp', 'dev')), may hold values from 128 to 256, as said below
- active_slot: int32 [32768], P(('grp', 'dev')), may hold values from 0 to 255, as said below
Outputs:
- pos_vel: float32 [6, 32768], P(None, ('grp', 'dev'))
- acc_jerk: float32 [6, 32768], P(None, ('grp', 'dev'))
- potential: float32 [32768], P(('grp', 'dev'))
Inputs may be any that keep to these rules, and one draw needn't show every extreme that they name: `live_count`: every entry is at least 128; some device is full with 256 and some has exactly 128; the counts are uneven across devices. `active_slot`: within each device's aligned block of 128 entries the slots are distinct and below that device's live_count.
All inputs are finite; a program needn't handle non-finite values.
Results may differ from a plain program's by a relative error of at most 0.00029.
Values sent between devices are 32-bit elements; how exact they have to be, the bound alone decides.
No kernel may reach another device: no remote copies, remote signals or barrier semaphores. Data moves between devices by JAX's collectives and lax.ppermute only.
A program may use at most 64 MiB of HBM per device.

v0:
```python
import jax
import jax.numpy as jnp
from jax import lax
from jax.sharding import PartitionSpec as P

tau_base = 0.5
soften_sq = 0.0001


def pair_terms(active_state, src_pos, src_vel, src_mass):
    delta_pos = src_pos[:, None, :] - active_state[0:3, :, None]
    delta_vel = src_vel[:, None, :] - active_state[3:6, :, None]
    dist_sq = jnp.sum(delta_pos * delta_pos, axis=0) + soften_sq
    weight = src_mass[None, :] / jnp.sqrt(dist_sq)
    cubed = weight / dist_sq
    radial = 3.0 * jnp.sum(delta_pos * delta_vel, axis=0) / dist_sq
    accel = jnp.sum(cubed[None] * delta_pos, axis=2)
    jerk_new = jnp.sum(cubed[None] * (delta_vel - radial[None] * delta_pos), axis=2)
    pot_sum = -jnp.sum(weight, axis=1)
    return jnp.concatenate([accel, jerk_new, pot_sum[None]], axis=0)


def correct(state, summed):
    pos_now = state[0:3]
    vel_now = state[3:6]
    acc_start = state[6:9]
    jerk_start = state[9:12]
    step_size = state[12:13]
    acc_end = summed[0:3]
    jerk_end = summed[3:6]
    differ = acc_start - acc_end
    fourth = -6.0 * differ - step_size * (4.0 * jerk_start + 2.0 * jerk_end)
    fifth = 12.0 * differ + 6.0 * step_size * (jerk_start + jerk_end)
    new_pos = (
        pos_now + step_size * step_size / 24.0 * fourth + step_size * step_size / 120.0 * fifth
    )
    new_vel = vel_now + step_size / 6.0 * fourth + step_size / 24.0 * fifth
    return (jnp.concatenate([new_pos, new_vel], axis=0), summed[0:6], summed[6])


def sweep_sources(active_state, pos_pred, vel_pred, live_mass):
    n_active = active_state.shape[1]
    block_size = min(512, n_active)
    blocks = active_state.reshape(6, n_active // block_size, block_size).transpose(1, 0, 2)

    def one_block(block):
        return pair_terms(block, pos_pred, vel_pred, live_mass)

    partial_value = lax.map(one_block, blocks)
    return partial_value.transpose(1, 0, 2).reshape(7, n_active)


def shards(positions, velocities, accel_old, jerk_old, masses, levels, live_count, active_slot):
    elapsed = tau_base * jnp.exp2(-levels.astype(jnp.float32))
    pos_pred = positions + elapsed * (
        velocities + elapsed * (accel_old / 2.0 + elapsed * jerk_old / 6.0)
    )
    vel_pred = velocities + elapsed * (accel_old + elapsed * jerk_old / 2.0)
    slots = jnp.arange(positions.shape[1], dtype=jnp.int32)
    live_mass = jnp.where(slots < live_count[0], masses, jnp.float32(0.0))
    owned = jnp.concatenate(
        [
            pos_pred[:, active_slot],
            vel_pred[:, active_slot],
            accel_old[:, active_slot],
            jerk_old[:, active_slot],
            elapsed[active_slot][None],
        ],
        axis=0,
    )
    active = lax.all_gather(owned[0:6], ("grp", "dev"), axis=1, tiled=True)
    partial_value = sweep_sources(active, pos_pred, vel_pred, live_mass)
    summed = lax.psum_scatter(partial_value, ("grp", "dev"), scatter_dimension=1, tiled=True)
    return correct(owned, summed)


def solution(mesh):
    return jax.shard_map(
        shards,
        mesh=mesh,
        in_specs=(
            P(None, ("grp", "dev")),
            P(None, ("grp", "dev")),
            P(None, ("grp", "dev")),
            P(None, ("grp", "dev")),
            P(("grp", "dev")),
            P(("grp", "dev")),
            P(("grp", "dev")),
            P(("grp", "dev")),
        ),
        out_specs=(P(None, ("grp", "dev")), P(None, ("grp", "dev")), P(("grp", "dev"))),
        check_vma=False,
    )
```

profile of v0, /device:TPU:0, one launch (start us, length us, event | category | flops | bytes accessed | tf_op | source)
XLA Modules:
  0.0 1480.0 jit_solution(7230137608994621387)
XLA Ops:
  11.1 64.7 %all_gather.3 = f32[6,32768]{1,0:T(8,128)S(1)} all-gather(f32[6,128]{1,0:T(8,128)S(1)} %pad_maximum_fusion), channel_id=1, replica_groups=mesh['grp'=4,'dev'=64] {'grp','dev'}, dimensions={1}, use_global_device_ids=true | all-gather | bytes 789504 | tf_op jit(solution)/shard_map/all_gather | solution.py:71
  76.5 109.0 %while.10 = (s32[]{:T(128)}, f32[64,7,512]{2,1,0:T(8,128)S(1)}, f32[256]{0:T(256)S(1)}, f32[3,256]{1,0:T(4,128)S(1)}, f32[64,6,512]{2,1,0:T(8,128)S(1)}, /*index...) while((s32[]{:T(128)}, f32[64,7,512]{2,1,0:T(8,128)S(1)}, f32[256]{0:T(256)S(1)}, f32[3,256]{1,0:T(4,128)S(1)}, ...), condition=%wide.region_6.7_spmd, body=%wide.region_0.6_spmd.sunk | while | flops 6033411 | bytes 4310133 | solution.py:49
  77.3 0.9 fusion.21
  79.0 0.9 fusion.21
  80.7 0.9 fusion.21
  82.4 0.9 fusion.21
  84.1 0.9 fusion.21
  85.8 0.9 fusion.21
  87.5 0.9 fusion.21
  89.2 0.9 fusion.21
  90.9 0.9 fusion.21
  92.6 0.9 fusion.21
  94.3 0.9 fusion.21
  96.0 0.9 fusion.21
  97.7 0.9 fusion.21
  99.4 0.9 fusion.21
  101.1 0.9 fusion.21
  102.8 0.9 fusion.21
  104.5 0.9 fusion.21
  106.2 0.9 fusion.21
  107.9 0.9 fusion.21
  109.6 0.9 fusion.21
  111.3 0.9 fusion.21
  113.0 0.9 fusion.21
  114.7 0.9 fusion.21
  116.4 0.9 fusion.21
  118.1 0.9 fusion.21
  119.8 0.9 fusion.21
  121.5 0.9 fusion.21
  123.2 0.9 fusion.21
  124.9 0.9 fusion.21
  126.6 0.9 fusion.21
  128.3 0.9 fusion.21
  130.0 0.9 fusion.21
  131.8 0.9 fusion.21
  133.5 0.9 fusion.21
  135.2 0.9 fusion.21
  136.9 0.9 fusion.21
  138.6 0.9 fusion.21
  140.3 0.9 fusion.21
  142.0 0.9 fusion.21
  143.7 0.9 fusion.21
  145.4 0.9 fusion.21
  147.1 0.9 fusion.21
  148.8 0.9 fusion.21
  153.9 0.9 fusion.21
  155.6 0.9 fusion.21
  157.3 0.9 fusion.21
  159.0 0.9 fusion.21
  160.7 0.9 fusion.21
  162.4 0.9 fusion.21
  164.1 0.9 fusion.21
  165.8 0.9 fusion.21
  170.9 0.9 fusion.21
  172.6 0.9 fusion.21
  174.3 0.9 fusion.21
  176.0 0.9 fusion.21
  177.7 0.9 fusion.21
  179.4 0.9 fusion.21
  181.1 0.9 fusion.21
  185.6 1.0 copy-done
  186.5 1.3 gather_fusion.1
  189.5 1281.0 %reduce-scatter.2.cloned.1.call-done = f32[7,128]{1,0:T(8,128)} async-done(((f32[7,32768]{1,0:T(8,128)}), f32[7,128]{1,0:T(8,128)}) %reduce-scatter.2.cloned.1.call-update) | async-done | bytes 3600 | tf_op jit(solution)/shard_map/reduce_scatter | solution.py:73
  1471.9 1.2 slice_bitcast_fusion
  (358 shorter events, 59.4 us)
Async XLA Ops:
  7.2 69.3 %copy-start.3 = (f32[256]{0:T(256)S(1)}, f32[256]{0:T(256)}, u32[]{:S(2)}) copy-start(f32[256]{0:T(256)} %param.14) | copy-start | bytes 3076
  7.2 1463.4 %reduce-scatter.2.cloned.1.call-start = ((), (), s32[]{:S(2)}) async-start(), calls=%async_computation.1 | async-start | bytes 1052672 | tf_op jit(solution)/shard_map/reduce_scatter | solution.py:73
  185.5 1.0 copy-start
  185.5 2.3 copy-start.1
  185.5 2.4 copy-start.2
Sparse Core Ops, SparseCore 0:
  186.7 1283.8 reduce-scatter.1
where the time goes:
time: 1480 us
  waiting for transfers between devices  1280 us (86%)
  other arithmetic  109 us (7%)
  blocking collectives  64.7 us (4%)
  between operations  14.8 us (1%)
    reduce_scatter x1, waiting for transfers between devices, shards(): lax.psum_scatter(partial_value, ('grp', 'dev'), scatter_dimension=1, tile...  1280 us
    all_gather x1, blocking collectives, shards(): active = lax.all_gather(owned[0:6], ('grp', 'dev'), axis=1, tiled=True)  64.7 us
    reduce_sum x64, other arithmetic, pair_terms(): accel = jnp.sum(cubed[None] * delta_pos, axis=2)  59.3 us
    reduce_sum x64, other arithmetic, pair_terms(): radial = 3.0 * jnp.sum(delta_pos * delta_vel, axis=0) / dist_sq  30.3 us
  transfers between devices with their start and end apart: 1, of which 1 were waited for; matrix products, arithmetic and copies ran while one was open for 0% of the time, Pallas kernels for 0%

commit v1 on v0

--- a/solution.py
+++ b/solution.py
@@ -68,7 +68,12 @@
         ],
         axis=0,
     )
-    active = lax.all_gather(owned[0:6], ("grp", "dev"), axis=1, tiled=True)
+    active = jnp.concatenate(
+        lax.all_to_all(
+            jnp.stack([owned[0:6]] * lax.axis_size(("grp", "dev"))), ("grp", "dev"), 0, 0
+        ),
+        axis=1,
+    )
     partial_value = sweep_sources(active, pos_pred, vel_pred, live_mass)
     summed = lax.psum_scatter(partial_value, ("grp", "dev"), scatter_dimension=1, tiled=True)
     return correct(owned, summed)

time: 1480 us -> 1460 us (0.986)
  blocking collectives: 64.7 us -> 0 us
  waiting for transfers between devices: 1280 us -> 1310 us
    all_gather x1 -> x0, blocking collectives: 64.7 us -> none  [shards(): active = lax.all_gather(owned[0:6], ('grp', 'dev'), axis=1, tiled=True)]
    all_to_all x0 -> x1, waiting for transfers between devices: none -> 28.4 us  [shards(): lax.all_to_all(jnp.stack([owned[0:6]] * lax.axis_size(('grp', 'dev'))), (...]
  transfers between devices with their start and end apart: 1 -> 2, of which waited for: 1 -> 2; matrix products, arithmetic and copies ran while one was open for 0% -> 0% of each run, Pallas kernels for 0% -> 0%
where the time goes in v1:
time: 1460 us
  waiting for transfers between devices  1310 us (90%)
  other arithmetic  109 us (7%)
  between operations  14.8 us (1%)
  starting transfers between devices  14.6 us (1%)
    reduce_scatter x1, waiting for transfers between devices, shards(): lax.psum_scatter(partial_value, ('grp', 'dev'), scatter_dimension=1, tile...  1280 us
    reduce_sum x64, other arithmetic, pair_terms(): accel = jnp.sum(cubed[None] * delta_pos, axis=2)  59.3 us
    reduce_sum x64, other arithmetic, pair_terms(): radial = 3.0 * jnp.sum(delta_pos * delta_vel, axis=0) / dist_sq  30.3 us
  transfers between devices with their start and end apart: 2, of which 2 were waited for; matrix products, arithmetic and copies ran while one was open for 0% of the time, Pallas kernels for 0%

profile of v1, /device:TPU:0, one launch (start us, length us, event | category | flops | bytes accessed | tf_op | source)
XLA Modules:
  0.0 1457.7 jit_solution(2480056466963752788)
XLA Ops:
  11.0 1.1 stack.2
  12.1 14.6 %all-to-all-start = ((f32[256,6,128]{2,1,0:T(8,128)}), f32[256,6,128]{2,1,0:T(8,128)S(1)}, u32[]{:S(2)}, u32[]{:S(2)}) async-start(f32[256,6,128]{2,1,0:T(8,128)} %stack.2), calls=%async_computation | async-start | bytes 2097152 | tf_op jit(solution)/shard_map/all_to_all | solution.py:72
  27.4 28.4 %all-to-all-done = f32[256,6,128]{2,1,0:T(8,128)S(1)} async-done(((f32[256,6,128]{2,1,0:T(8,128)}), f32[256,6,128]{2,1,0:T(8,128)S(1)}, u32[]{:S(2)}, u32[]{:S(2)}) %all-to-all-start) | async-done | bytes 786464 | tf_op jit(solution)/shard_map/all_to_all | solution.py:72
  55.8 108.8 %while.10 = (s32[]{:T(128)}, f32[64,7,512]{2,1,0:T(8,128)S(1)}, f32[256]{0:T(256)S(1)}, f32[3,256]{1,0:T(4,128)S(1)}, f32[64,6,512]{2,1,0:T(8,128)S(1)}, /*index...) while((s32[]{:T(128)}, f32[64,7,512]{2,1,0:T(8,128)S(1)}, f32[256]{0:T(256)S(1)}, f32[3,256]{1,0:T(4,128)S(1)}, ...), condition=%wide.region_6.7_spmd, body=%wide.region_0.6_spmd.sunk | while | flops 6033411 | bytes 4310133 | solution.py:49
  56.6 0.9 fusion.21
  58.3 0.9 fusion.21
  60.0 0.9 fusion.21
  61.7 0.9 fusion.21
  63.4 0.9 fusion.21
  65.1 0.9 fusion.21
  66.8 0.9 fusion.21
  68.5 0.9 fusion.21
  70.2 0.9 fusion.21
  71.9 0.9 fusion.21
  73.6 0.9 fusion.21
  75.3 0.9 fusion.21
  77.0 0.9 fusion.21
  78.7 0.9 fusion.21
  80.4 0.9 fusion.21
  82.1 0.9 fusion.21
  83.8 0.9 fusion.21
  85.5 0.9 fusion.21
  87.2 0.9 fusion.21
  88.9 0.9 fusion.21
  90.6 0.9 fusion.21
  92.3 0.9 fusion.21
  94.0 0.9 fusion.21
  95.7 0.9 fusion.21
  97.4 0.9 fusion.21
  99.1 0.9 fusion.21
  100.8 0.9 fusion.21
  102.5 0.9 fusion.21
  104.2 0.9 fusion.21
  105.9 0.9 fusion.21
  107.6 0.9 fusion.21
  109.3 0.9 fusion.21
  111.0 0.9 fusion.21
  112.7 0.9 fusion.21
  114.4 0.9 fusion.21
  117.8 0.9 fusion.21
  119.5 0.9 fusion.21
  122.9 0.9 fusion.21
  124.6 0.9 fusion.21
  128.0 0.9 fusion.21
  129.7 0.9 fusion.21
  133.1 0.9 fusion.21
  134.8 0.9 fusion.21
  136.5 0.9 fusion.21
  138.2 0.9 fusion.21
  139.9 0.9 fusion.21
  141.6 0.9 fusion.21
  143.3 0.9 fusion.21
  145.0 0.9 fusion.21
  146.7 0.9 fusion.21
  150.1 0.9 fusion.21
  151.8 0.9 fusion.21
  155.2 0.9 fusion.21
  156.9 0.9 fusion.21
  160.3 0.9 fusion.21
  162.0 0.9 fusion.21
  164.7 1.0 copy-done
  165.7 1.3 gather_fusion.1
  168.7 1279.6 %reduce-scatter.2.cloned.1.call-done = f32[7,128]{1,0:T(8,128)} async-done(((f32[7,32768]{1,0:T(8,128)}), f32[7,128]{1,0:T(8,128)}) %reduce-scatter.2.cloned.1.call-update) | async-done | bytes 3600 | tf_op jit(solution)/shard_map/reduce_scatter | solution.py:78
  1449.7 1.2 slice_bitcast_fusion
  (360 shorter events, 61.1 us)
Async XLA Ops:
  12.1 15.3 %copy-start.3 = (f32[256]{0:T(256)S(1)}, f32[256]{0:T(256)}, u32[]{:S(2)}) copy-start(f32[256]{0:T(256)} %param.14) | copy-start | bytes 3076
  12.1 43.7 %all-to-all-start = ((f32[256,6,128]{2,1,0:T(8,128)}), f32[256,6,128]{2,1,0:T(8,128)S(1)}, u32[]{:S(2)}, u32[]{:S(2)}) async-start(f32[256,6,128]{2,1,0:T(8,128)} %stack.2), calls=%async_computation | async-start | bytes 2097152 | tf_op jit(solution)/shard_map/all_to_all | solution.py:72
  26.7 1421.6 %reduce-scatter.2.cloned.1.call-start = ((), (), s32[]{:S(2)}) async-start(), calls=%async_computation.2 | async-start | bytes 1052672 | tf_op jit(solution)/shard_map/reduce_scatter | solution.py:78
  164.7 1.0 copy-start
  164.7 2.3 copy-start.1
  164.7 2.4 copy-start.2
Sparse Core Ops, SparseCore 0:
  165.8 1282.4 reduce-scatter.1
